TPU v7x, 512 devices: a whole 4x8x8 slice. The times are simulated.
512 devices in a mesh: lat: 32 (over x_hi, z, core), lon: 16 (over y, x_lo).
Axes of the slice: x: 4 (x_hi: 2, x_lo: 2; x = x_hi * 2 + x_lo), y: 8, z: 8, core: 2. Of those that a mesh axis runs over, the one named last changes fastest.
Arguments:
- nodes: bfloat16 [32, 16, 128, 512], P('lat', 'lon'), may hold values from -6 to 6
- top_nodes: bfloat16 [1024, 512], P('lat'), may hold values from -6 to 6
- cotangent: bfloat16 [32, 16, 128, 512], P('lat', 'lon'), may hold values from -3 to 3
- w_src: bfloat16 [512, 512], replicated, may hold values from -0.25 to 0.25
- w_dst: bfloat16 [512, 512], replicated, may hold values from -0.25 to 0.25
- w_msg: bfloat16 [512, 512], replicated, may hold values from -0.25 to 0.25
- w_top: bfloat16 [512, 512], replicated, may hold values from -0.25 to 0.25
- src_code: int32 [32, 16, 1024], P('lat', 'lon'), may hold values from 0 to 8
- src_node: int32 [32, 16, 1024], P('lat', 'lon'), may hold values from 0 to 127
- dst_node: int32 [32, 16, 1024], P('lat', 'lon'), may hold values from 0 to 127
- edge_count: int32 [32, 16], P('lat', 'lon'), may hold values from 256 to 1024, as said below
- parent: int32 [32, 16, 128], P('lat', 'lon'), may hold values from 0 to 1023, as said below
Outputs:
- updated: bfloat16 [32, 16, 128, 512], P('lat', 'lon')
- weight_grads: bfloat16 [4, 512, 512], replicated
- d_top: bfloat16 [1024, 512], P(('lat', 'lon'))
Inputs may be any that keep to these rules, and one draw needn't show every extreme that they name: `edge_count`: some block has all 1024 slots live. Top-level nodes come in bands of 32, one band for the one block row. Node n of block (i, j) lies at longitude position p = j * 128 + n, and c = p * 32 // 2048 is the band column above it. Its parent is (i) * 32 + k for a column k of 0 to 31 with |k - c| <= 2.
All inputs are finite; a program needn't handle non-finite values.
Results may differ from a plain program's by a relative error of at most 0.006.
Values may be sent and summed in bfloat16 or wider, within the bound.
No kernel may reach another device: no remote copies, remote signals or barrier semaphores. Data moves between devices by JAX's collectives and lax.ppermute only.
A program may use at most 64 MiB of HBM per device.

v0:
```python
import math
import jax
import jax.numpy as jnp
from jax import lax
from jax.sharding import PartitionSpec as P


def extended_2(block, sides, width):
    for axis, dim in sides:
        count = lax.axis_size(axis)
        forward = [(i, i + 1) for i in range(count - 1)]
        backward = [(target, source) for source, target in forward]
        low = lax.ppermute(
            lax.slice_in_dim(block, block.shape[dim] - width, None, axis=dim), axis, forward
        )
        high = lax.ppermute(lax.slice_in_dim(block, 0, width, axis=dim), axis, backward)
        block = jnp.concatenate([low, block, high], axis=dim)
    return block


def silu_slope(values):
    sigmoid_v = jax.nn.sigmoid(values)
    return sigmoid_v * (1.0 + values * (1.0 - sigmoid_v))


def contract_rows(left_mat, right_mat):
    return lax.dot_general(
        left_mat, right_mat, (((0,), (0,)), ((), ())), preferred_element_type=jnp.float32
    )


def shards(
    nodes,
    top_nodes,
    cotangent,
    w_src,
    w_dst,
    w_msg,
    w_top,
    src_code,
    src_node,
    dst_node,
    edge_count,
    parent,
):
    block_rows, block_cols, block_size, features = nodes.shape
    block_count = block_rows * block_cols
    slot_count = src_code.shape[-1]
    ext_cols = block_cols + 2
    top_local = top_nodes.shape[0]
    owner_rows = top_local // lax.axis_size("lon")
    lon_index = lax.axis_index("lon")
    band_start = lax.axis_index("lat") * top_local
    parents = parent.reshape(-1)
    band_ids = parents - band_start
    window_ids = band_ids - (lon_index - 1) * owner_rows
    top_table = jnp.dot(top_nodes, w_top, preferred_element_type=jnp.float32).astype(jnp.bfloat16)
    table_rows = jnp.take(top_table, band_ids, axis=0)
    extended = extended_2(nodes, (("lat", 0), ("lon", 1)), 1)
    ext_flat = extended.reshape(-1, features)
    src_proj = jnp.dot(ext_flat, w_src, preferred_element_type=jnp.float32)
    local_rows = nodes.reshape(-1, features)
    dst_proj = jnp.dot(local_rows, w_dst, preferred_element_type=jnp.float32)
    block_row = lax.iota(jnp.int32, block_rows)[:, None, None]
    block_col = lax.iota(jnp.int32, block_cols)[None, :, None]
    src_idx = (
        ((block_row + src_code // 3) * ext_cols + block_col + src_code % 3) * block_size + src_node
    ).reshape(-1)
    dst_idx = ((block_row * block_cols + block_col) * block_size + dst_node).reshape(-1)
    live_slot = lax.iota(jnp.int32, slot_count)[None, None, :] < edge_count[:, :, None]
    node_ids = lax.iota(jnp.int32, block_size)[None, :, None]
    one_hot = ((dst_node == node_ids) & live_slot).astype(jnp.bfloat16)
    pre_act = jnp.take(src_proj, src_idx, axis=0) + jnp.take(dst_proj, dst_idx, axis=0)
    hidden = jax.nn.silu(pre_act).astype(jnp.bfloat16)
    msg_pre = jnp.dot(hidden, w_msg, preferred_element_type=jnp.float32)
    message = jax.nn.silu(msg_pre).astype(jnp.bfloat16)
    inflow = jnp.einsum(
        "bne,bed->bnd",
        one_hot,
        message.reshape(block_count, slot_count, features),
        preferred_element_type=jnp.float32,
    ).reshape(-1, features)
    node_pre = inflow + table_rows.astype(jnp.float32)
    updated = (
        (local_rows.astype(jnp.float32) + jax.nn.silu(node_pre))
        .astype(jnp.bfloat16)
        .reshape(nodes.shape)
    )
    node_grad = (cotangent.reshape(-1, features).astype(jnp.float32) * silu_slope(node_pre)).astype(
        jnp.bfloat16
    )
    msg_grad = jnp.einsum(
        "bne,bnd->bed",
        one_hot,
        node_grad.reshape(block_count, block_size, features),
        preferred_element_type=jnp.float32,
    ).reshape(-1, features)
    pre_grad = (msg_grad * silu_slope(msg_pre)).astype(jnp.bfloat16)
    grad_msg = contract_rows(hidden, pre_grad)
    hidden_grad = lax.dot_general(
        pre_grad, w_msg, (((1,), (1,)), ((), ())), preferred_element_type=jnp.float32
    )
    act_grad = (hidden_grad * silu_slope(pre_act)).astype(jnp.bfloat16)
    dst_grad = (
        jnp.einsum(
            "bne,bed->bnd",
            one_hot,
            act_grad.reshape(block_count, slot_count, features),
            preferred_element_type=jnp.float32,
        )
        .astype(jnp.bfloat16)
        .reshape(-1, features)
    )
    grad_dst = contract_rows(local_rows, dst_grad)
    grad_src = contract_rows(jnp.take(ext_flat, src_idx, axis=0), act_grad)
    window_cols = lax.iota(jnp.int32, 3 * owner_rows)
    picks = (window_ids[:, None] == window_cols[None, :]).astype(jnp.bfloat16)
    window_sum = contract_rows(picks, node_grad)
    rims = jnp.concatenate([window_sum[:owner_rows], window_sum[2 * owner_rows :]], axis=0)
    rim_parts = extended_2(rims, (("lon", 0),), owner_rows)
    table_sum = (
        window_sum[owner_rows : 2 * owner_rows]
        + rim_parts[:owner_rows]
        + rim_parts[3 * owner_rows :]
    )
    table_grad = table_sum.astype(jnp.bfloat16)
    top_mine = lax.dynamic_slice_in_dim(top_nodes, lon_index * owner_rows, owner_rows, 0)
    d_top = lax.dot_general(
        table_grad, w_top, (((1,), (1,)), ((), ())), preferred_element_type=jnp.float32
    ).astype(jnp.bfloat16)
    grad_top = contract_rows(top_mine, table_grad)
    summed = lax.psum((grad_src, grad_dst, grad_msg, grad_top), ("lat", "lon"))
    nodes_total = block_count * block_size * lax.axis_size("lat") * lax.axis_size("lon")
    grad_scale = 8.0 / math.sqrt(nodes_total)
    weight_grads = (jnp.stack(summed) * grad_scale).astype(jnp.bfloat16)
    return (updated, weight_grads, d_top)


def solution(mesh):
    placed = (
        P("lat", "lon", None, None),
        P("lat", None),
        P("lat", "lon", None, None),
        P(),
        P(),
        P(),
        P(),
        P("lat", "lon", None),
        P("lat", "lon", None),
        P("lat", "lon", None),
        P("lat", "lon"),
        P("lat", "lon", None),
    )
    return jax.shard_map(
        shards,
        mesh=mesh,
        in_specs=placed,
        out_specs=(P("lat", "lon", None, None), P(), P(("lat", "lon"), None)),
        check_vma=False,
    )
```

profile of v0, /device:TPU:17, one launch (start us, length us, event | category | flops | bytes accessed | tf_op | source)
XLA Modules:
  0.0 388.7 jit_solution(804594889232757917)
XLA Ops:
  7.2 0.0 copy-start
  7.2 0.0 all-reduce.3.cloned.1.call-start
  7.2 2.7 collective-permute-start.1
  9.9 3.9 %collective-permute-start = (bf16[1,1,128,512]{3,2,1,0:T(8,128)(2,1)}, bf16[1,1,128,512]{3,2,1,0:T(8,128)(2,1)S(1)}, u32[]{:S(2)}, u32[]{:S(2)}) collective-permute-start(bf16[1,1,128,512]{3,2,1,0:T(8,128)(2,1)} %param.12), channel_id=1, source_target_pairs={{0,16},{16,32},{32,48},{48,64},{64,80},{80,96},{96,112},{112,128},... | collective-permute-start | bytes 393224 | tf_op jit(solution)/shard_map/ppermute | solution.py:13
  13.9 0.7 compare_select_fusion
  14.6 0.7 compare_select_fusion.1
  15.3 1.3 fusion.20
  16.7 0.7 fusion.28
  17.3 1.2 convolution_convert_fusion.1
  18.6 1.3 compare_and_fusion.2
  20.5 1.5 gather_fusion.2
  22.0 4.9 %gather_fusion.1 = f32[1024,512]{1,0:T(8,128)} fusion(f32[128,512]{1,0:T(8,128)S(1)} %fusion.20, s32[1024]{0:T(1024)S(1)} %get-tuple-element.14), kind=kCustom, calls=%fused_computation.1 | custom fusion | bytes 4198400 | tf_op jit(solution)/shard_map/jit(_take)/gather | solution.py:73
  26.9 0.6 iota_compare_fusion.3
  27.4 0.0 collective-permute-done
  27.4 0.0 copy-done.5
  27.5 0.0 collective-permute-done.1
  27.5 3.0 collective-permute-start.3
  30.5 2.3 collective-permute-start.2
  32.8 0.0 copy-done.12
  32.8 0.5 bitcast_subtract_fusion
  33.3 0.0 copy-done.10
  33.4 14.3 %collective-permute-done.3 = bf16[3,1,128,512]{3,2,1,0:T(8,128)(2,1)S(1)} collective-permute-done((bf16[3,1,128,512]{3,2,1,0:T(8,128)(2,1)S(1)}, bf16[3,1,128,512]{3,2,1,0:T(8,128)(2,1)S(1)}, u32[]{:S(2)}, u32[]{:S(2)}) %collective-permute-start.3) | collective-permute-done | bytes 393248 | tf_op jit(solution)/shard_map/ppermute | solution.py:16
  47.7 0.3 collective-permute-done.2
  47.9 0.1 pad_maximum_fusion
  48.1 0.0 copy-start.1
  48.1 1.0 copy-done.1
  49.1 5.1 %gather_fusion.3 = bf16[1024,512]{1,0:T(8,128)(2,1)} fusion(bf16[1152,512]{1,0:T(8,128)(2,1)S(1)} %bitcast.58, s32[1024]{0:T(1024)S(1)} %broadcast_clamp_fusion.1), kind=kCustom, calls=%fused_computation.3 | custom fusion | bytes 2101248 | tf_op jit(solution)/shard_map/jit(_take)/gather | solution.py:115
  54.2 0.0 copy-done.7
  54.2 2.0 fusion.33
  56.2 4.9 %gather_fusion = f32[1024,512]{1,0:T(8,128)} fusion(f32[1152,512]{1,0:T(8,128)S(1)} %fusion.33, s32[1024]{0:T(1024)S(1)} %broadcast_clamp_fusion.1), kind=kCustom, calls=%fused_computation | custom fusion | bytes 4198400 | tf_op jit(solution)/shard_map/jit(_take)/gather | solution.py:73
  61.1 2.6 multiply_convert_fusion.3
  63.7 0.0 copy-done
  63.8 0.0 copy-start.8
  63.8 0.0 copy-start.11
  63.8 0.0 copy-start.14
  63.8 0.7 fusion.34
  64.5 0.2 copy-done.8
  64.7 0.0 copy-done.11
  64.7 0.0 copy-done.14
  64.7 1.5 fusion.10
  66.1 0.0 copy-done.9
  66.1 0.1 fusion.9
  66.3 0.0 copy-start.2
  66.3 0.0 copy-start.3
  66.3 0.9 multiply_convert_fusion.1
  67.2 0.7 copy-done.2
  67.8 0.6 copy-done.3
  68.5 1.6 multiply_convert_fusion
  70.1 0.0 copy-start.13
  70.1 0.0 copy-start.6
  70.1 1.7 convolution_bitcast_fusion.1
  71.9 0.2 fusion.22
  72.1 4.0 %collective-permute-start.4 = (f32[2,512]{1,0:T(2,128)S(1)}, f32[2,512]{1,0:T(2,128)S(1)}, u32[]{:S(2)}, u32[]{:S(2)}) collective-permute-start(f32[2,512]{1,0:T(2,128)S(1)} %get-tuple-element.9), channel_id=1, source_target_pairs={{0,1},{1,2},{2,3},{3,4},{4,5},{5,6},{6,7},{7,8},{8,9},{9,10},{10,1... | collective-permute-start | bytes 12296 | tf_op jit(solution)/shard_map/ppermute | solution.py:13
  76.1 2.2 collective-permute-start.5
  78.3 1.8 convolution_bitcast_fusion.3
  80.1 1.6 convolution_bitcast_fusion.2
  81.7 0.0 collective-permute-done.4
  81.7 0.0 collective-permute-done.5
  81.7 2.0 convolution_bitcast_fusion
  83.8 0.0 all-reduce.3.cloned.1.call-update
  83.8 1.0 copy-done.4
  84.8 0.8 convolution_convert_fusion.2
  85.6 292.2 %all-reduce.3.cloned.1.call-done = (f32[1,512,512]{2,1,0:T(8,128)}, f32[1,512,512]{2,1,0:T(8,128)}, f32[1,512,512]{2,1,0:T(8,128)}, f32[1,512,512]{2,1,0:T(8,128)}) async-done(((f32[1,512,512]{2,1,0:T(8,128)}, f32[1,512,512]{2,1,0:T(8,128)}, f32[1,512,512]{2,1,0:T(8,128)}, f32[1,512,512]{2,1,0:T(8,128)}), (f32[1,512,512]{2,1,0:T(8,128)}, f32[1,512,512]{2,1,0:T(8,128)}, f32[1,512,512]{2,1,0:T(8,128)}, ...) | async-done | bytes 4194320 | tf_op jit(solution)/shard_map/psum | solution.py:132
  377.8 4.1 %fusion = bf16[4,512,512]{2,1,0:T(8,128)(2,1)} fusion(f32[1,512,512]{2,1,0:T(8,128)} %get-tuple-element.3, f32[1,512,512]{2,1,0:T(8,128)} %get-tuple-element.4, f32[1,512,512]{2,1,0:T(8,128)} %get-tuple-element.5, f32[1,512,512]{2,1,0:T(8,128)} %get-tuple-element.6), kind=kLoop, calls=%fused_computation.5 | loop fusion | flops 5242880 | bytes 6291456 | tf_op jit(solution)/shard_map/convert_element_type | solution.py:135
  (16 shorter events, 0.1 us)
Async XLA Ops:
  7.2 56.6 %copy-start = (bf16[512,512]{1,0:T(8,128)(2,1)S(1)}, bf16[512,512]{1,0:T(8,128)(2,1)}, u32[]{:S(2)}) copy-start(bf16[512,512]{1,0:T(8,128)(2,1)} %param.17) | copy-start | bytes 1572868
  7.2 370.6 %all-reduce.3.cloned.1.call-start = ((), (), s32[]{:S(2)}) async-start(), calls=%async_computation | async-start | bytes 8388608 | tf_op jit(solution)/shard_map/psum | solution.py:132
  7.2 20.3 %collective-permute-start.1 = (bf16[1,1,128,512]{3,2,1,0:T(8,128)(2,1)}, bf16[1,1,128,512]{3,2,1,0:T(8,128)(2,1)S(1)}, u32[]{:S(2)}, u32[]{:S(2)}) collective-permute-start(bf16[1,1,128,512]{3,2,1,0:T(8,128)(2,1)} %param.12), channel_id=1, source_target_pairs={{16,0},{32,16},{48,32},{64,48},{80,64},{96,80},{112,96},{128,112},... | collective-permute-start | bytes 393224 | tf_op jit(solution)/shard_map/ppermute | solution.py:16
  9.9 17.5 %collective-permute-start = (bf16[1,1,128,512]{3,2,1,0:T(8,128)(2,1)}, bf16[1,1,128,512]{3,2,1,0:T(8,128)(2,1)S(1)}, u32[]{:S(2)}, u32[]{:S(2)}) collective-permute-start(bf16[1,1,128,512]{3,2,1,0:T(8,128)(2,1)} %param.12), channel_id=1, source_target_pairs={{0,16},{16,32},{32,48},{48,64},{64,80},{80,96},{96,112},{112,128},... | collective-permute-start | bytes 393224 | tf_op jit(solution)/shard_map/ppermute | solution.py:13
  22.0 5.5 %copy-start.5 = (bf16[1,1,128,512]{3,2,1,0:T(8,128)(2,1)S(1)}, bf16[1,1,128,512]{3,2,1,0:T(8,128)(2,1)}, u32[]{:S(2)}) copy-start(bf16[1,1,128,512]{3,2,1,0:T(8,128)(2,1)} %param.12) | copy-start | bytes 393220
  22.0 10.8 %copy-start.12 = (s32[1,1,128]{2,1,0:T(1,128)S(1)}, s32[1,1,128]{2,1,0:T(1,128)}, u32[]{:S(2)}) copy-start(s32[1,1,128]{2,1,0:T(1,128)} %param.23) | copy-start | bytes 1540
  22.0 11.3 %copy-start.10 = (s32[1,1,1024]{2,1,0:T(1,128)S(1)}, s32[1,1,1024]{2,1,0:T(1,128)}, u32[]{:S(2)}) copy-start(s32[1,1,1024]{2,1,0:T(1,128)} %param.21) | copy-start | bytes 12292
  27.5 20.1 %collective-permute-start.3 = (bf16[3,1,128,512]{3,2,1,0:T(8,128)(2,1)S(1)}, bf16[3,1,128,512]{3,2,1,0:T(8,128)(2,1)S(1)}, u32[]{:S(2)}, u32[]{:S(2)}) collective-permute-start(bf16[3,1,128,512]{3,2,1,0:T(8,128)(2,1)S(1)} %constant_dynamic-update-slice_fusion), channel_id=1, source_target_pairs={{1,0},{2,1},{3,2},{4,3},{5,4},{6,5},{7,6},{8,7},{9,8},{10,9},{11,1... | collective-permute-start | bytes 1179656 | tf_op jit(solution)/shard_map/ppermute | solution.py:16
  30.5 17.4 %collective-permute-start.2 = (bf16[3,1,128,512]{3,2,1,0:T(8,128)(2,1)S(1)}, bf16[3,1,128,512]{3,2,1,0:T(8,128)(2,1)S(1)}, u32[]{:S(2)}, u32[]{:S(2)}) collective-permute-start(bf16[3,1,128,512]{3,2,1,0:T(8,128)(2,1)S(1)} %constant_dynamic-update-slice_fusion), channel_id=1, source_target_pairs={{0,1},{1,2},{2,3},{3,4},{4,5},{5,6},{6,7},{7,8},{8,9},{9,10},{10,1... | collective-permute-start | bytes 1179656 | tf_op jit(solution)/shard_map/ppermute | solution.py:13
  48.1 1.0 copy-start.1
  49.1 5.1 %copy-start.7 = (bf16[512,512]{1,0:T(8,128)(2,1)S(1)}, bf16[512,512]{1,0:T(8,128)(2,1)}, u32[]{:S(2)}) copy-start(bf16[512,512]{1,0:T(8,128)(2,1)} %param.15) | copy-start | bytes 1572868
  63.8 0.9 copy-start.8
  63.8 0.9 copy-start.11
  63.8 0.9 copy-start.14
  64.7 1.5 copy-start.9
  66.3 1.6 copy-start.2
  66.3 2.2 copy-start.3
  70.1 1.8 copy-start.13
  70.1 8.2 %copy-start.6 = (bf16[1024,512]{1,0:T(8,128)(2,1)S(1)}, bf16[1024,512]{1,0:T(8,128)(2,1)}, u32[]{:S(2)}) copy-start(bf16[1024,512]{1,0:T(8,128)(2,1)} %gather_fusion.3) | copy-start | bytes 3145732
  72.1 9.6 %collective-permute-start.4 = (f32[2,512]{1,0:T(2,128)S(1)}, f32[2,512]{1,0:T(2,128)S(1)}, u32[]{:S(2)}, u32[]{:S(2)}) collective-permute-start(f32[2,512]{1,0:T(2,128)S(1)} %get-tuple-element.9), channel_id=1, source_target_pairs={{0,1},{1,2},{2,3},{3,4},{4,5},{5,6},{6,7},{7,8},{8,9},{9,10},{10,1... | collective-permute-start | bytes 12296 | tf_op jit(solution)/shard_map/ppermute | solution.py:13
  76.1 5.6 %collective-permute-start.5 = (f32[2,512]{1,0:T(2,128)S(1)}, f32[2,512]{1,0:T(2,128)S(1)}, u32[]{:S(2)}, u32[]{:S(2)}) collective-permute-start(f32[2,512]{1,0:T(2,128)S(1)} %get-tuple-element.10), channel_id=1, source_target_pairs={{1,0},{2,1},{3,2},{4,3},{5,4},{6,5},{7,6},{8,7},{9,8},{10,9},{11,1... | collective-permute-start | bytes 12296 | tf_op jit(solution)/shard_map/ppermute | solution.py:16
  83.7 1.0 copy-start.4
Sparse Core Ops, SparseCore 0:
  83.9 293.8 all-reduce.2
where the time goes:
time: 389 us
  waiting for transfers between devices  307 us (79%)
  local copies, waits for them, and re-layouts  19.9 us (5%)
  starting transfers between devices  18.1 us (5%)
  matrix products  17.5 us (4%)
  between operations  14.9 us (4%)
  other arithmetic  11.4 us (3%)
    psum x1, waiting for transfers between devices, shards(): summed = lax.psum((grad_src, grad_dst, grad_msg, grad_top), ('lat', 'lon'))  292 us
    ppermute x3, waiting for transfers between devices, extended_2(): lax.ppermute(lax.slice_in_dim(block, 0, width, axis=dim), axis, backward)  14.3 us
    ppermute x3, starting transfers between devices, extended_2(): lax.ppermute(lax.slice_in_dim(block, block.shape[dim] - width, None, axis...  10.2 us
    ppermute x3, starting transfers between devices, extended_2(): lax.ppermute(lax.slice_in_dim(block, 0, width, axis=dim), axis, backward)  7.93 us
  transfers between devices with their start and end apart: 7, of which 3 were waited for; matrix products, arithmetic and copies ran while one was open for 5% of the time, Pallas kernels for 0%

commit v1 on v0

--- a/solution.py
+++ b/solution.py
@@ -129,7 +129,7 @@
         table_grad, w_top, (((1,), (1,)), ((), ())), preferred_element_type=jnp.float32
     ).astype(jnp.bfloat16)
     grad_top = contract_rows(top_mine, table_grad)
-    summed = lax.psum((grad_src, grad_dst, grad_msg, grad_top), ("lat", "lon"))
+    summed = lax.psum(lax.psum((grad_src, grad_dst, grad_msg, grad_top), "lat"), "lon")
     nodes_total = block_count * block_size * lax.axis_size("lat") * lax.axis_size("lon")
     grad_scale = 8.0 / math.sqrt(nodes_total)
     weight_grads = (jnp.stack(summed) * grad_scale).astype(jnp.bfloat16)

time: 389 us -> 598 us (1.54)
  the two profiles are of different devices: /device:TPU:17 before, /device:TPU:10 now
where the time goes in v1:
time: 598 us; the launch traced here: 597 us
  waiting for transfers between devices  516 us (86%)
  local copies, waits for them, and re-layouts  19.9 us (3%)
  matrix products  17.5 us (3%)
  starting transfers between devices  17.1 us (3%)
  between operations  15 us (3%)
  other arithmetic  11.4 us (2%)
    psum x1, waiting for transfers between devices, shards(): lax.psum((grad_src, grad_dst, grad_msg, grad_top), 'lat')  290 us
    psum x1, waiting for transfers between devices, shards(): lax.psum(lax.psum((grad_src, grad_dst, grad_msg, grad_top), 'lat'), 'lon')  210 us
    ppermute x3, waiting for transfers between devices, extended_2(): lax.ppermute(lax.slice_in_dim(block, 0, width, axis=dim), axis, backward)  12 us
  transfers between devices with their start and end apart: 8, of which 4 were waited for; matrix products, arithmetic and copies ran while one was open for 3% of the time, Pallas kernels for 0%

profile of v1, /device:TPU:10, one launch (start us, length us, event | category | flops | bytes accessed | tf_op | source)
XLA Modules:
  0.0 597.3 jit_solution(7446669781996171863)
XLA Ops:
  7.2 0.0 copy-start
  7.2 0.0 all-reduce.5.cloned.1.call-start
  7.2 1.4 collective-permute-start.1
  8.7 3.0 collective-permute-start
  11.7 0.7 compare_select_fusion
  12.4 0.7 compare_select_fusion.1
  13.2 1.3 fusion.21
  14.5 0.7 fusion.30
  15.2 1.2 convolution_convert_fusion.1
  16.4 1.3 compare_and_fusion.2
  18.4 1.5 gather_fusion.2
  19.9 4.9 gather_fusion.1
  24.7 0.6 iota_compare_fusion.3
  25.3 0.0 collective-permute-done
  25.3 0.0 copy-done.5
  25.3 0.0 collective-permute-done.1
  25.4 2.4 collective-permute-start.3
  27.8 4.3 collective-permute-start.2
  32.1 0.0 copy-done.12
  32.1 0.5 bitcast_subtract_fusion
  32.7 0.0 copy-done.10
  32.7 12.0 %collective-permute-done.3 = bf16[3,1,128,512]{3,2,1,0:T(8,128)(2,1)S(1)} collective-permute-done((bf16[3,1,128,512]{3,2,1,0:T(8,128)(2,1)S(1)}, bf16[3,1,128,512]{3,2,1,0:T(8,128)(2,1)S(1)}, u32[]{:S(2)}, u32[]{:S(2)}) %collective-permute-start.3) | collective-permute-done | bytes 393248 | tf_op jit(solution)/shard_map/ppermute | solution.py:16
  44.7 3.8 collective-permute-done.2
  48.5 0.1 pad_maximum_fusion
  48.6 0.0 copy-start.1
  48.7 1.0 copy-done.1
  49.7 5.1 gather_fusion.3
  54.7 2.0 fusion.35
  56.8 4.9 gather_fusion
  61.7 2.6 multiply_convert_fusion.3
  64.3 0.0 copy-start.8
  64.3 0.0 copy-start.11
  64.4 0.0 copy-start.14
  64.4 0.7 fusion.36
  65.1 0.2 copy-done.8
  65.2 0.0 copy-done.14
  65.3 1.5 fusion.11
  66.7 0.0 copy-done.9
  66.7 0.1 fusion.10
  66.8 0.0 copy-start.2
  66.9 0.9 multiply_convert_fusion.1
  67.8 0.7 copy-done.2
  68.4 0.6 copy-done.3
  69.1 1.6 multiply_convert_fusion
  70.7 0.0 copy-start.13
  70.7 0.0 copy-start.6
  70.7 1.7 fusion.37
  72.4 0.0 copy-done.13
  72.5 0.2 fusion.23
  72.7 2.5 collective-permute-start.4
  75.2 3.4 collective-permute-start.5
  78.6 1.8 fusion.1
  80.4 1.6 convolution_bitcast_fusion
  81.9 0.0 collective-permute-done.4
  81.9 0.0 collective-permute-done.5
  82.0 2.0 fusion.28
  84.0 0.0 all-reduce.5.cloned.1.call-update
  84.0 0.0 all-reduce.7.cloned.1.call-start
  84.1 290.3 %all-reduce.5.cloned.1.call-done = (f32[512,512]{1,0:T(8,128)}, f32[512,512]{1,0:T(8,128)}, f32[512,512]{1,0:T(8,128)}, f32[512,512]{1,0:T(8,128)}) async-done(((f32[512,512]{1,0:T(8,128)}, f32[512,512]{1,0:T(8,128)}, f32[512,512]{1,0:T(8,128)}, f32[512,512]{1,0:T(8,128)}), (f32[512,512]{1,0:T(8,128)}, f32[512,512]{1,0:T(8,128)}, f32[512,512]{1,0:T(8,128)}, ...) | async-done | bytes 4194320 | tf_op jit(solution)/shard_map/psum | solution.py:132
  374.3 0.0 all-reduce.7.cloned.1.call-update
  374.4 1.0 copy-done.4
  375.4 0.8 convolution_convert_fusion.2
  376.2 210.2 %all-reduce.7.cloned.1.call-done = (f32[1,512,512]{2,1,0:T(8,128)}, f32[1,512,512]{2,1,0:T(8,128)}, f32[1,512,512]{2,1,0:T(8,128)}, f32[1,512,512]{2,1,0:T(8,128)}) async-done(((f32[1,512,512]{2,1,0:T(8,128)}, f32[1,512,512]{2,1,0:T(8,128)}, f32[1,512,512]{2,1,0:T(8,128)}, f32[1,512,512]{2,1,0:T(8,128)}), (f32[1,512,512]{2,1,0:T(8,128)}, f32[1,512,512]{2,1,0:T(8,128)}, f32[1,512,512]{2,1,0:T(8,128)}, ...) | async-done | bytes 4194320 | tf_op jit(solution)/shard_map/psum | solution.py:132
  586.4 4.1 fusion
  (19 shorter events, 0.1 us)
Async XLA Ops:
  7.2 57.2 %copy-start = (bf16[512,512]{1,0:T(8,128)(2,1)S(1)}, bf16[512,512]{1,0:T(8,128)(2,1)}, u32[]{:S(2)}) copy-start(bf16[512,512]{1,0:T(8,128)(2,1)} %param.17) | copy-start | bytes 1572868
  7.2 367.2 %all-reduce.5.cloned.1.call-start = ((), (), s32[]{:S(2)}) async-start(), calls=%async_computation | async-start | bytes 8388608 | tf_op jit(solution)/shard_map/psum | solution.py:132
  7.2 18.1 %collective-permute-start.1 = (bf16[1,1,128,512]{3,2,1,0:T(8,128)(2,1)}, bf16[1,1,128,512]{3,2,1,0:T(8,128)(2,1)S(1)}, u32[]{:S(2)}, u32[]{:S(2)}) collective-permute-start(bf16[1,1,128,512]{3,2,1,0:T(8,128)(2,1)} %param.12), channel_id=1, source_target_pairs={{16,0},{32,16},{48,32},{64,48},{80,64},{96,80},{112,96},{128,112},... | collective-permute-start | bytes 393224 | tf_op jit(solution)/shard_map/ppermute | solution.py:16
  8.7 16.6 %collective-permute-start = (bf16[1,1,128,512]{3,2,1,0:T(8,128)(2,1)}, bf16[1,1,128,512]{3,2,1,0:T(8,128)(2,1)S(1)}, u32[]{:S(2)}, u32[]{:S(2)}) collective-permute-start(bf16[1,1,128,512]{3,2,1,0:T(8,128)(2,1)} %param.12), channel_id=1, source_target_pairs={{0,16},{16,32},{32,48},{48,64},{64,80},{80,96},{96,112},{112,128},... | collective-permute-start | bytes 393224 | tf_op jit(solution)/shard_map/ppermute | solution.py:13
  19.9 5.5 copy-start.5
  19.9 12.3 %copy-start.12 = (s32[1,1,128]{2,1,0:T(1,128)S(1)}, s32[1,1,128]{2,1,0:T(1,128)}, u32[]{:S(2)}) copy-start(s32[1,1,128]{2,1,0:T(1,128)} %param.23) | copy-start | bytes 1540
  19.9 12.8 %copy-start.10 = (s32[1,1,1024]{2,1,0:T(1,128)S(1)}, s32[1,1,1024]{2,1,0:T(1,128)}, u32[]{:S(2)}) copy-start(s32[1,1,1024]{2,1,0:T(1,128)} %param.21) | copy-start | bytes 12292
  25.4 19.3 %collective-permute-start.3 = (bf16[3,1,128,512]{3,2,1,0:T(8,128)(2,1)S(1)}, bf16[3,1,128,512]{3,2,1,0:T(8,128)(2,1)S(1)}, u32[]{:S(2)}, u32[]{:S(2)}) collective-permute-start(bf16[3,1,128,512]{3,2,1,0:T(8,128)(2,1)S(1)} %constant_dynamic-update-slice_fusion), channel_id=1, source_target_pairs={{1,0},{2,1},{3,2},{4,3},{5,4},{6,5},{7,6},{8,7},{9,8},{10,9},{11,1... | collective-permute-start | bytes 1179656 | tf_op jit(solution)/shard_map/ppermute | solution.py:16
  27.8 20.7 %collective-permute-start.2 = (bf16[3,1,128,512]{3,2,1,0:T(8,128)(2,1)S(1)}, bf16[3,1,128,512]{3,2,1,0:T(8,128)(2,1)S(1)}, u32[]{:S(2)}, u32[]{:S(2)}) collective-permute-start(bf16[3,1,128,512]{3,2,1,0:T(8,128)(2,1)S(1)} %constant_dynamic-update-slice_fusion), channel_id=1, source_target_pairs={{0,1},{1,2},{2,3},{3,4},{4,5},{5,6},{6,7},{7,8},{8,9},{9,10},{10,1... | collective-permute-start | bytes 1179656 | tf_op jit(solution)/shard_map/ppermute | solution.py:13
  48.6 1.0 copy-start.1
  49.7 5.1 copy-start.7
  64.3 0.9 copy-start.8
  64.3 0.9 copy-start.11
  64.4 0.9 copy-start.14
  65.2 1.5 copy-start.9
  66.8 1.6 copy-start.2
  66.8 2.2 copy-start.3
  70.7 1.8 copy-start.13
  70.7 7.9 %copy-start.6 = (bf16[1024,512]{1,0:T(8,128)(2,1)S(1)}, bf16[1024,512]{1,0:T(8,128)(2,1)}, u32[]{:S(2)}) copy-start(bf16[1024,512]{1,0:T(8,128)(2,1)} %gather_fusion.3) | copy-start | bytes 3145732
  72.7 9.2 %collective-permute-start.4 = (f32[2,512]{1,0:T(2,128)S(1)}, f32[2,512]{1,0:T(2,128)S(1)}, u32[]{:S(2)}, u32[]{:S(2)}) collective-permute-start(f32[2,512]{1,0:T(2,128)S(1)} %get-tuple-element.13), channel_id=1, source_target_pairs={{0,1},{1,2},{2,3},{3,4},{4,5},{5,6},{6,7},{7,8},{8,9},{9,10},{10,1... | collective-permute-start | bytes 12296 | tf_op jit(solution)/shard_map/ppermute | solution.py:13
  75.2 6.8 %collective-permute-start.5 = (f32[2,512]{1,0:T(2,128)S(1)}, f32[2,512]{1,0:T(2,128)S(1)}, u32[]{:S(2)}, u32[]{:S(2)}) collective-permute-start(f32[2,512]{1,0:T(2,128)S(1)} %get-tuple-element.14), channel_id=1, source_target_pairs={{1,0},{2,1},{3,2},{4,3},{5,4},{6,5},{7,6},{8,7},{9,8},{10,9},{11,1... | collective-permute-start | bytes 12296 | tf_op jit(solution)/shard_map/ppermute | solution.py:16
  84.0 502.4 %all-reduce.7.cloned.1.call-start = ((), (), s32[]{:S(2)}) async-start(), calls=%async_computation.1 | async-start | bytes 8388608 | tf_op jit(solution)/shard_map/psum | solution.py:132
  374.3 1.0 copy-start.4
Sparse Core Ops, SparseCore 0:
  84.1 290.1 all-reduce.4
  377.5 208.8 all-reduce.6
